TPU v7x, 32 devices: a whole 2x2x4 slice. The times are simulated.
32 devices in a mesh: bus: 8 (over y, x, core), period: 4 (over z).
Axes of the slice: x: 2, y: 2, z: 4, core: 2. Of those that a mesh axis runs over, the one named last changes fastest.
Arguments:
- deviation: bfloat16 [128, 256, 128], P('bus', 'period'), may hold values from -6 to 6
- loading: bfloat16 [128, 256, 128], P('bus', 'period'), may hold values from 0.5 to 2
- jacobian: bfloat16 [128, 128, 128], P('bus'), may hold values from -0.5 to 0.5
- tie_source: int32 [128, 16], P('bus'), may hold values from 0 to 127
- tie_target: int32 [128, 16], P('bus'), may hold values from 0 to 127
- tie_admittance: float32 [128, 16], P('bus'), may hold values from 0.5 to 2
- condense: bfloat16 [128, 128, 512], P('bus'), may hold values from -0.046875 to 0.046875
- section_gain: bfloat16 [4, 64, 512, 512], P('period', 'bus'), may hold values from -0.0625 to 0.0625
- retention: float32 [4, 64, 512], P('period', 'bus'), may hold values from 0 to 1
Outputs:
- mismatch: bfloat16 [128, 256, 128], P('bus', 'period')
- section_states: float32 [4, 64, 512], P('period', 'bus')
All inputs are finite; a program needn't handle non-finite values.
Results may differ from a plain program's by a relative error of at most 0.013.
Values may be sent and summed in bfloat16 or wider, within the bound.
No kernel may reach another device: no remote copies, remote signals or barrier semaphores. Data moves between devices by JAX's collectives and lax.ppermute only.
A program may use at most 64 MiB of HBM per device.

v0:
```python
import jax
import jax.numpy as jnp
from jax import lax
from jax.sharding import PartitionSpec as P


def from_behind(value, axis, steps):
    count = lax.axis_size(axis)
    leading, last = (max(0, -steps), min(count, count - steps))
    return lax.ppermute(value, axis, [(source, source + steps) for source in range(leading, last)])


def entering_2(value, axis, combine, identity):
    size, place = (lax.axis_size(axis), lax.axis_index(axis))
    everything = jax.tree.map(lambda part: lax.all_gather(part, axis), value)
    start = jax.tree.map(
        lambda part, zero: jnp.broadcast_to(jnp.asarray(zero, part.dtype), part.shape),
        value,
        identity,
    )

    def step(k, before):
        reached = k < place
        new = combine(before, jax.tree.map(lambda part: part[k], everything))
        return jax.tree.map(lambda a, b: jnp.where(reached, a, b), new, before)

    return lax.fori_loop(0, size, step, start)


def broadcast(block, axis, owner):
    block = jnp.where(lax.axis_index(axis) == owner, block, jnp.zeros_like(block))
    return lax.psum(block, axis)


def combine(earlier, later):
    return (earlier[0] * later[0], later[0] * earlier[1] + later[1])


def place(flows, hot):
    upper = flows.astype(jnp.bfloat16)
    lower = (flows - upper.astype(jnp.float32)).astype(jnp.bfloat16)
    both = jnp.concatenate([upper, lower], axis=2)
    hot_twice = jnp.concatenate([hot, hot], axis=1)
    return jnp.einsum("bte,beq->btq", both, hot_twice, preferred_element_type=jnp.float32)


def shards(
    deviation,
    loading,
    jacobian,
    tie_source,
    tie_target,
    tie_admittance,
    condense,
    section_gain,
    retention,
):
    block_width = deviation.shape[2]
    scaled = (deviation.astype(jnp.float32) * loading.astype(jnp.float32)).astype(jnp.bfloat16)
    columns = jnp.arange(block_width, dtype=jnp.int32)
    source_hot = (tie_source[:, :, None] == columns[None, None, :]).astype(jnp.bfloat16)
    target_hot = (tie_target[:, :, None] == columns[None, None, :]).astype(jnp.bfloat16)
    next_first = from_behind(scaled[0], "bus", -1)
    next_block = jnp.concatenate([scaled[1:], next_first[None]], axis=0)
    at_target = jnp.einsum(
        "btq,beq->bte", next_block, target_hot, preferred_element_type=jnp.float32
    )
    network = jnp.einsum("btp,bpq->btq", scaled, jacobian, preferred_element_type=jnp.float32)
    at_source = jnp.einsum("btq,beq->bte", scaled, source_hot, preferred_element_type=jnp.float32)
    edge_flow = tie_admittance[:, None, :] * (at_target - at_source)
    own_terms = place(edge_flow, source_hot)
    handed = -place(edge_flow, target_hot)
    incoming = from_behind(handed[-1], "bus", 1)
    received = jnp.concatenate([incoming[None], handed[:-1]], axis=0)
    mismatch = (network + own_terms + received).astype(jnp.bfloat16)
    span_rows = section_gain.shape[1]
    partial_value = jnp.einsum(
        "btq,bqm->tm", mismatch, condense, preferred_element_type=jnp.float32
    )
    totals = lax.psum(partial_value, "bus")
    section_sum = lax.dynamic_slice_in_dim(totals, lax.axis_index("bus") * span_rows, span_rows, 0)
    section_in = section_sum.astype(jnp.bfloat16)
    pushed = jnp.einsum(
        "tm,tmn->tn", section_in, section_gain[0], preferred_element_type=jnp.float32
    )
    states_width = pushed.shape[1]
    ones_row = jnp.ones((states_width,), jnp.float32)
    zeros_row = jnp.zeros((states_width,), jnp.float32)

    def advance(carried, inputs):
        section_now, product = carried
        retain, pushed_now = inputs
        section_now = retain * section_now + pushed_now
        product = product * retain
        return ((section_now, product), (section_now, product))

    (last_state, span_rate), (local_states, running) = lax.scan(
        advance, (zeros_row, ones_row), (retention[0], pushed)
    )
    own_map = (span_rate, last_state)
    identity = (ones_row, zeros_row)
    before = entering_2(own_map, "bus", combine, identity)
    through = combine(before, own_map)
    group_map = (
        broadcast(through[0], "bus", lax.axis_size("bus") - 1),
        broadcast(through[1], "bus", lax.axis_size("bus") - 1),
    )
    across = entering_2(group_map, "period", combine, identity)
    entering = combine(across, before)[1]
    states = local_states + running * entering[None, :]
    return (mismatch, states[None])


def solution(mesh):
    placed = (
        P("bus", "period", None),
        P("bus", "period", None),
        P("bus", None, None),
        P("bus", None),
        P("bus", None),
        P("bus", None),
        P("bus", None, None),
        P("period", "bus", None, None),
        P("period", "bus", None),
    )
    return jax.shard_map(
        shards,
        mesh=mesh,
        in_specs=placed,
        out_specs=(P("bus", "period", None), P("period", "bus", None)),
        check_vma=False,
    )
```

profile of v0, /device:TPU:0, one launch (start us, length us, event | category | flops | bytes accessed | tf_op | source)
XLA Modules:
  0.0 106.2 jit_solution(14670595446566683150)
XLA Ops:
  0.7 1.3 %multiply_convert_fusion = bf16[16,64,128]{2,1,0:T(8,128)(2,1)S(1)} fusion(bf16[16,64,128]{2,1,0:T(8,128)(2,1)} %param.16, bf16[16,64,128]{2,1,0:T(8,128)(2,1)} %param.15), kind=kLoop, calls=%fused_computation.21 | loop fusion | flops 524288 | bytes 786432 | tf_op jit(solution)/shard_map/convert_element_type | solution.py:59
  1.9 1.3 %collective-permute-start = (bf16[64,128]{1,0:T(8,128)(2,1)S(1)}, bf16[64,128]{1,0:T(8,128)(2,1)S(1)}, u32[]{:S(2)}, u32[]{:S(2)}) collective-permute-start(bf16[64,128]{1,0:T(8,128)(2,1)S(1)} %slice_bitcast_fusion.1), channel_id=1, source_target_pairs={{4,0},{8,4},{12,8},{16,12},{20,16},{24,20},{28,24},{5,1},{9,5},{13... | collective-permute-start | bytes 49160 | tf_op jit(solution)/shard_map/ppermute | solution.py:10
  3.2 1.0 fusion.23
  4.2 1.3 %fusion.25 = f32[16,64,128]{2,1,0:T(8,128)S(1)} fusion(bf16[16,64,128]{2,1,0:T(8,128)(2,1)S(1)} %multiply_convert_fusion, bf16[16,128,128]{2,1,0:T(8,128)(2,1)} %param.17), kind=kOutput, calls=%fused_computation.56 | convolution fusion | flops 33554432 | bytes 1310720 | tf_op jit(solution)/shard_map/btp,bpq->btq/dot_general | solution.py:68
  5.5 0.8 iota_compare_fusion.1
  6.4 1.0 fusion.24
  7.7 3.8 %collective-permute-start.1 = (f32[64,128]{1,0:T(8,128)S(1)}, f32[64,128]{1,0:T(8,128)S(1)}, u32[]{:S(2)}, u32[]{:S(2)}) collective-permute-start(f32[64,128]{1,0:T(8,128)S(1)} %slice_bitcast_fusion), channel_id=1, source_target_pairs={{0,4},{4,8},{8,12},{12,16},{16,20},{20,24},{24,28},{1,5},{5,9},{9,... | collective-permute-start | bytes 98312 | tf_op jit(solution)/shard_map/ppermute | solution.py:10
  13.2 26.5 %all-reduce.2 = bf16[64,512]{1,0:T(8,128)(2,1)S(1)} all-reduce(f32[64,512]{1,0:T(8,128)S(1)} %convolution_bitcast_fusion), channel_id=1, replica_groups=mesh['bus'=8,'period'=4] {'bus'}, use_global_device_ids=true, to_apply=%region_0.0 | all-reduce | flops 32768 | bytes 196608 | tf_op jit(solution)/shard_map/psum | solution.py:80
  39.7 2.8 %fusion.1 = f32[8,1,512]{2,1,0:T(1,128)S(1)} fusion(bf16[1,8,512,512]{3,2,1,0:T(8,128)(2,1)} %param.22, bf16[8,512,1]{1,0,2:T(8,128)(2,1)S(1)} %fusion.17), kind=kOutput, calls=%fused_computation.12 | convolution fusion | flops 4194304 | bytes 4218880 | tf_op jit(solution)/shard_map/tm,tmn->tn/dot_general | solution.py:83
  42.5 7.1 %while.47 = (s32[]{:T(128)}, f32[512]{0:T(512)S(1)}, f32[512]{0:T(512)S(1)}, f32[8,512]{1,0:T(8,128)S(1)}, f32[8,512]{1,0:T(8,128)S(1)}, /*index=5*/f32[8,512]{1...) while((s32[]{:T(128)}, f32[512]{0:T(512)S(1)}, f32[512]{0:T(512)S(1)}, f32[8,512]{1,0:T(8,128)S(1)}, ...), condition=%wide.region_2.3_spmd.clone, body=%wide.region_1.2_spmd.clone.sunk | while | flops 2563 | bytes 28787 | solution.py:97
  42.5 0.7 constant_dynamic-slice_fusion.9
  43.4 0.7 constant_dynamic-slice_fusion.9
  44.3 0.7 constant_dynamic-slice_fusion.9
  45.2 0.7 constant_dynamic-slice_fusion.9
  46.1 0.7 constant_dynamic-slice_fusion.9
  47.0 0.7 constant_dynamic-slice_fusion.9
  47.9 0.7 constant_dynamic-slice_fusion.9
  48.8 0.7 constant_dynamic-slice_fusion.9
  49.7 10.4 %all-gather.3 = f32[8,1,512]{2,1,0:T(1,128)S(1)} all-gather(f32[1,1,512]{2,1,0:T(1,128)S(1)} %bitcast.67), channel_id=3, replica_groups=mesh['bus'=8,'period'=4] {'bus'}, dimensions={0}, use_global_device_ids=true | all-gather | bytes 18432 | tf_op jit(solution)/shard_map/all_gather | solution.py:15
  60.0 7.7 %all-gather.2 = f32[8,1,512]{2,1,0:T(1,128)S(1)} all-gather(f32[1,1,512]{2,1,0:T(1,128)S(1)} %bitcast.69), channel_id=2, replica_groups=mesh['bus'=8,'period'=4] {'bus'}, dimensions={0}, use_global_device_ids=true | all-gather | bytes 18432 | tf_op jit(solution)/shard_map/all_gather | solution.py:15
  68.2 13.2 %all-reduce = (f32[1,512]{1,0:T(1,128)S(1)}, f32[1,512]{1,0:T(1,128)S(1)}) all-reduce(f32[1,512]{1,0:T(1,128)S(1)} %bitcast.83, f32[1,512]{1,0:T(1,128)S(1)} %bitcast.82), channel_id=1, replica_groups=mesh['bus'=8,'period'=4] {'bus'}, use_global_device_ids=true, to_apply=%region_5.6 | all-reduce | flops 1024 | bytes 8192 | tf_op jit(solution)/shard_map/psum | solution.py:32
  81.4 12.1 %all-gather.5 = f32[4,1,512]{2,1,0:T(1,128)S(1)} all-gather(f32[1,1,512]{2,1,0:T(1,128)S(1)} %bitcast.86), channel_id=1, replica_groups=mesh['bus'=8,'period'=4] {'period'}, dimensions={0}, use_global_device_ids=true | all-gather | bytes 10240 | tf_op jit(solution)/shard_map/all_gather | solution.py:15
  93.5 11.9 %all-gather.4 = f32[4,1,512]{2,1,0:T(1,128)S(1)} all-gather(f32[1,1,512]{2,1,0:T(1,128)S(1)} %bitcast.85), channel_id=1, replica_groups=mesh['bus'=8,'period'=4] {'period'}, dimensions={0}, use_global_device_ids=true | all-gather | bytes 10240 | tf_op jit(solution)/shard_map/all_gather | solution.py:15
  105.6 0.6 add_bitcast_fusion
  (81 shorter events, 3.8 us)
Async XLA Ops:
  0.6 12.0 %copy-start = (bf16[16,128,512]{2,1,0:T(8,128)(2,1)S(1)}, bf16[16,128,512]{2,1,0:T(8,128)(2,1)}, u32[]{:S(2)}) copy-start(bf16[16,128,512]{2,1,0:T(8,128)(2,1)} %param.21) | copy-start | bytes 6291460
  0.6 10.9 %copy-start.2 = (s32[16,16]{1,0:T(8,128)S(1)}, s32[16,16]{1,0:T(8,128)}, u32[]{:S(2)}) copy-start(s32[16,16]{1,0:T(8,128)} %param.18) | copy-start | bytes 3076
  1.9 4.5 %collective-permute-start = (bf16[64,128]{1,0:T(8,128)(2,1)S(1)}, bf16[64,128]{1,0:T(8,128)(2,1)S(1)}, u32[]{:S(2)}, u32[]{:S(2)}) collective-permute-start(bf16[64,128]{1,0:T(8,128)(2,1)S(1)} %slice_bitcast_fusion.1), channel_id=1, source_target_pairs={{4,0},{8,4},{12,8},{16,12},{20,16},{24,20},{28,24},{5,1},{9,5},{13... | collective-permute-start | bytes 49160 | tf_op jit(solution)/shard_map/ppermute | solution.py:10
  7.7 4.7 %collective-permute-start.1 = (f32[64,128]{1,0:T(8,128)S(1)}, f32[64,128]{1,0:T(8,128)S(1)}, u32[]{:S(2)}, u32[]{:S(2)}) collective-permute-start(f32[64,128]{1,0:T(8,128)S(1)} %slice_bitcast_fusion), channel_id=1, source_target_pairs={{0,4},{4,8},{8,12},{12,16},{16,20},{20,24},{24,28},{1,5},{5,9},{9,... | collective-permute-start | bytes 98312 | tf_op jit(solution)/shard_map/ppermute | solution.py:10
  12.7 93.5 %copy-start.1 = (bf16[16,64,128]{2,1,0:T(8,128)(2,1)}, bf16[16,64,128]{2,1,0:T(8,128)(2,1)S(1)}, u32[]{:S(2)}) copy-start(bf16[16,64,128]{2,1,0:T(8,128)(2,1)S(1)} %fusion.4) | copy-start | bytes 786436
where the time goes:
time: 107 us; the launch traced here: 106 us
  blocking collectives  81.7 us (76%)
  matrix products  7.18 us (7%)
  local copies, waits for them, and re-layouts  7.02 us (7%)
  starting transfers between devices  5.11 us (5%)
  other arithmetic  3.07 us (3%)
    all_gather x4, blocking collectives, entering_2(): everything = jax.tree.map(lambda part: lax.all_gather(part, axis), value)  42 us
    psum x1, blocking collectives, shards(): totals = lax.psum(partial_value, 'bus')  26.5 us
    psum x1, blocking collectives, broadcast(): return lax.psum(block, axis)  13.2 us
    dynamic_slice x8, local copies, waits for them, and re-layouts, shards(): lax.scan(advance, (zeros_row, ones_row), (retention[0], pushed))  5.84 us
    ppermute x2, starting transfers between devices, from_behind(): lax.ppermute(value, axis, [(source, source + steps) for source in range(l...  5.11 us
    dot_general x1, matrix products, shards(): jnp.einsum('tm,tmn->tn', section_in, section_gain[0], preferred_element_t...  2.83 us
  transfers between devices with their start and end apart: 2, of which 1 were waited for; matrix products, arithmetic and copies ran while one was open for 3% of the time, Pallas kernels for 0%

commit v1 on v0

--- a/solution.py
+++ b/solution.py
@@ -2,6 +2,7 @@
 import jax.numpy as jnp
 from jax import lax
 from jax.sharding import PartitionSpec as P
+from jax.lax import all_gather
 
 
 def from_behind(value, axis, steps):
@@ -77,7 +78,7 @@
     partial_value = jnp.einsum(
         "btq,bqm->tm", mismatch, condense, preferred_element_type=jnp.float32
     )
-    totals = lax.psum(partial_value, "bus")
+    totals = jnp.sum(all_gather(partial_value, "bus"), axis=0)
     section_sum = lax.dynamic_slice_in_dim(totals, lax.axis_index("bus") * span_rows, span_rows, 0)
     section_in = section_sum.astype(jnp.bfloat16)
     pushed = jnp.einsum(

time: 107 us -> 123 us (1.15)
  waiting for transfers between devices: 0.6 us -> 29 us
  blocking collectives: 81.7 us -> 53.8 us
  between operations: 0.9 us -> 14.3 us
  other arithmetic: 3.07 us -> 4.38 us
    all_gather x0 -> x1, waiting for transfers between devices: none -> 28.3 us  [shards(): totals = jnp.sum(all_gather(partial_value, 'bus'), axis=0)]
    psum x1 -> x0, blocking collectives: 26.5 us -> none  [shards(): totals = lax.psum(partial_value, 'bus')]
    all_gather x4, blocking collectives: 42 us -> 40.6 us  [entering_2(): everything = jax.tree.map(lambda part: lax.all_gather(part, axis), value)]
    reduce_sum x0 -> x1, other arithmetic: none -> 1.32 us  [shards(): totals = jnp.sum(all_gather(partial_value, 'bus'), axis=0)]
  transfers between devices with their start and end apart: 2 -> 3, of which waited for: 1 -> 2; matrix products, arithmetic and copies ran while one was open for 3% -> 3% of each run, Pallas kernels for 0% -> 0%
where the time goes in v1:
time: 123 us; the launch traced here: 122 us
  blocking collectives  53.8 us (44%)
  waiting for transfers between devices  29 us (24%)
  between operations  14.3 us (12%)
  matrix products  7.84 us (6%)
  local copies, waits for them, and re-layouts  7.02 us (6%)
  starting transfers between devices  5.15 us (4%)
  other arithmetic  4.38 us (4%)
    all_gather x4, blocking collectives, entering_2(): everything = jax.tree.map(lambda part: lax.all_gather(part, axis), value)  40.6 us
    all_gather x1, waiting for transfers between devices, shards(): totals = jnp.sum(all_gather(partial_value, 'bus'), axis=0)  28.3 us
    psum x1, blocking collectives, broadcast(): return lax.psum(block, axis)  13.2 us
    dynamic_slice x8, local copies, waits for them, and re-layouts, shards(): lax.scan(advance, (zeros_row, ones_row), (retention[0], pushed))  5.84 us
    ppermute x2, starting transfers between devices, from_behind(): lax.ppermute(value, axis, [(source, source + steps) for source in range(l...  5.11 us
    dot_general x1, matrix products, shards(): jnp.einsum('tm,tmn->tn', section_in, section_gain[0], preferred_element_t...  2.83 us
  transfers between devices with their start and end apart: 3, of which 2 were waited for; matrix products, arithmetic and copies ran while one was open for 3% of the time, Pallas kernels for 0%

profile of v1, /device:TPU:0, one launch (start us, length us, event | category | flops | bytes accessed | tf_op | source)
XLA Modules:
  0.0 122.0 jit_solution(301412429448031556)
XLA Ops:
  7.2 1.2 %multiply_convert_fusion = bf16[16,64,128]{2,1,0:T(8,128)(2,1)S(1)} fusion(bf16[16,64,128]{2,1,0:T(8,128)(2,1)} %param.16, bf16[16,64,128]{2,1,0:T(8,128)(2,1)} %param.15), kind=kLoop, calls=%fused_computation.21 | loop fusion | flops 524288 | bytes 786432 | tf_op jit(solution)/shard_map/convert_element_type | solution.py:60
  8.5 1.3 %collective-permute-start = (bf16[64,128]{1,0:T(8,128)(2,1)S(1)}, bf16[64,128]{1,0:T(8,128)(2,1)S(1)}, u32[]{:S(2)}, u32[]{:S(2)}) collective-permute-start(bf16[64,128]{1,0:T(8,128)(2,1)S(1)} %slice_bitcast_fusion.1), channel_id=1, source_target_pairs={{4,0},{8,4},{12,8},{16,12},{20,16},{24,20},{28,24},{5,1},{9,5},{13... | collective-permute-start | bytes 49160 | tf_op jit(solution)/shard_map/ppermute | solution.py:11
  9.8 1.0 fusion.23
  10.8 1.3 %fusion.25 = f32[16,64,128]{2,1,0:T(8,128)S(1)} fusion(bf16[16,64,128]{2,1,0:T(8,128)(2,1)S(1)} %multiply_convert_fusion, bf16[16,128,128]{2,1,0:T(8,128)(2,1)} %param.17), kind=kOutput, calls=%fused_computation.56 | convolution fusion | flops 33554432 | bytes 1310720 | tf_op jit(solution)/shard_map/btp,bpq->btq/dot_general | solution.py:69
  12.1 0.8 iota_compare_fusion.1
  13.0 1.0 fusion.24
  14.3 3.8 %collective-permute-start.1 = (f32[64,128]{1,0:T(8,128)S(1)}, f32[64,128]{1,0:T(8,128)S(1)}, u32[]{:S(2)}, u32[]{:S(2)}) collective-permute-start(f32[64,128]{1,0:T(8,128)S(1)} %slice_bitcast_fusion), channel_id=1, source_target_pairs={{0,4},{4,8},{8,12},{12,16},{16,20},{20,24},{24,28},{1,5},{5,9},{9,... | collective-permute-start | bytes 98312 | tf_op jit(solution)/shard_map/ppermute | solution.py:11
  19.2 1.1 convolution_bitcast_fusion
  20.5 28.3 %all-gather.9.cloned.1.call-done = f32[512,512]{1,0:T(8,128)} async-done(((f32[64,512]{1,0:T(8,128)}), f32[512,512]{1,0:T(8,128)}) %all-gather.9.cloned.1.call-update) | async-done | bytes 1048592 | tf_op jit(solution)/shard_map/all_gather | solution.py:81
  48.8 1.3 %reduce_sum.9 = bf16[64,512]{1,0:T(8,128)(2,1)S(1)} reduce(f32[8,64,512]{2,1,0:T(8,128)} %bitcast.67, f32[]{:T(128)} %constant.70.clone.1), dimensions={0}, to_apply=%region_0.0 | reduce | flops 229376 | bytes 1114116 | tf_op jit(solution)/shard_map/reduce_sum | solution.py:81
  50.1 2.8 %fusion.1 = f32[8,1,512]{2,1,0:T(1,128)S(1)} fusion(bf16[1,8,512,512]{3,2,1,0:T(8,128)(2,1)} %param.22, bf16[8,512,1]{1,0,2:T(8,128)(2,1)S(1)} %fusion.17), kind=kOutput, calls=%fused_computation.12 | convolution fusion | flops 4194304 | bytes 4218880 | tf_op jit(solution)/shard_map/tm,tmn->tn/dot_general | solution.py:84
  52.9 7.1 %while.47 = (s32[]{:T(128)}, f32[512]{0:T(512)S(1)}, f32[512]{0:T(512)S(1)}, f32[8,512]{1,0:T(8,128)S(1)}, f32[8,512]{1,0:T(8,128)S(1)}, /*index=5*/f32[8,512]{1...) while((s32[]{:T(128)}, f32[512]{0:T(512)S(1)}, f32[512]{0:T(512)S(1)}, f32[8,512]{1,0:T(8,128)S(1)}, ...), condition=%wide.region_2.3_spmd.clone, body=%wide.region_1.2_spmd.clone.sunk | while | flops 2563 | bytes 28787 | solution.py:98
  52.9 0.7 constant_dynamic-slice_fusion.9
  53.9 0.7 constant_dynamic-slice_fusion.9
  54.7 0.7 constant_dynamic-slice_fusion.9
  55.6 0.7 constant_dynamic-slice_fusion.9
  56.5 0.7 constant_dynamic-slice_fusion.9
  57.4 0.7 constant_dynamic-slice_fusion.9
  59.2 0.7 constant_dynamic-slice_fusion.9
  60.1 8.9 %all-gather.4 = f32[8,1,512]{2,1,0:T(1,128)S(1)} all-gather(f32[1,1,512]{2,1,0:T(1,128)S(1)} %bitcast.69), channel_id=4, replica_groups=mesh['bus'=8,'period'=4] {'bus'}, dimensions={0}, use_global_device_ids=true | all-gather | bytes 18432 | tf_op jit(solution)/shard_map/all_gather | solution.py:16
  69.0 7.9 %all-gather.3 = f32[8,1,512]{2,1,0:T(1,128)S(1)} all-gather(f32[1,1,512]{2,1,0:T(1,128)S(1)} %bitcast.71), channel_id=3, replica_groups=mesh['bus'=8,'period'=4] {'bus'}, dimensions={0}, use_global_device_ids=true | all-gather | bytes 18432 | tf_op jit(solution)/shard_map/all_gather | solution.py:16
  77.4 13.2 %all-reduce = (f32[1,512]{1,0:T(1,128)S(1)}, f32[1,512]{1,0:T(1,128)S(1)}) all-reduce(f32[1,512]{1,0:T(1,128)S(1)} %bitcast.85, f32[1,512]{1,0:T(1,128)S(1)} %bitcast.84), channel_id=1, replica_groups=mesh['bus'=8,'period'=4] {'bus'}, use_global_device_ids=true, to_apply=%region_5.6 | all-reduce | flops 1024 | bytes 8192 | tf_op jit(solution)/shard_map/psum | solution.py:33
  90.5 11.9 %all-gather.6 = f32[4,1,512]{2,1,0:T(1,128)S(1)} all-gather(f32[1,1,512]{2,1,0:T(1,128)S(1)} %bitcast.88), channel_id=1, replica_groups=mesh['bus'=8,'period'=4] {'period'}, dimensions={0}, use_global_device_ids=true | all-gather | bytes 10240 | tf_op jit(solution)/shard_map/all_gather | solution.py:16
  102.5 11.9 %all-gather.5 = f32[4,1,512]{2,1,0:T(1,128)S(1)} all-gather(f32[1,1,512]{2,1,0:T(1,128)S(1)} %bitcast.87), channel_id=1, replica_groups=mesh['bus'=8,'period'=4] {'period'}, dimensions={0}, use_global_device_ids=true | all-gather | bytes 10240 | tf_op jit(solution)/shard_map/all_gather | solution.py:16
  (84 shorter events, 4.8 us)
Async XLA Ops:
  7.2 12.1 %copy-start = (bf16[16,128,512]{2,1,0:T(8,128)(2,1)S(1)}, bf16[16,128,512]{2,1,0:T(8,128)(2,1)}, u32[]{:S(2)}) copy-start(bf16[16,128,512]{2,1,0:T(8,128)(2,1)} %param.21) | copy-start | bytes 6291460
  7.2 10.9 %copy-start.2 = (s32[16,16]{1,0:T(8,128)S(1)}, s32[16,16]{1,0:T(8,128)}, u32[]{:S(2)}) copy-start(s32[16,16]{1,0:T(8,128)} %param.18) | copy-start | bytes 3076
  7.2 41.6 %all-gather.9.cloned.1.call-start = ((), (), s32[]{:S(2)}) async-start(), calls=%async_computation | async-start | bytes 1179648 | tf_op jit(solution)/shard_map/all_gather | solution.py:81
  8.5 4.5 %collective-permute-start = (bf16[64,128]{1,0:T(8,128)(2,1)S(1)}, bf16[64,128]{1,0:T(8,128)(2,1)S(1)}, u32[]{:S(2)}, u32[]{:S(2)}) collective-permute-start(bf16[64,128]{1,0:T(8,128)(2,1)S(1)} %slice_bitcast_fusion.1), channel_id=1, source_target_pairs={{4,0},{8,4},{12,8},{16,12},{20,16},{24,20},{28,24},{5,1},{9,5},{13... | collective-permute-start | bytes 49160 | tf_op jit(solution)/shard_map/ppermute | solution.py:11
  14.3 4.7 %collective-permute-start.1 = (f32[64,128]{1,0:T(8,128)S(1)}, f32[64,128]{1,0:T(8,128)S(1)}, u32[]{:S(2)}, u32[]{:S(2)}) collective-permute-start(f32[64,128]{1,0:T(8,128)S(1)} %slice_bitcast_fusion), channel_id=1, source_target_pairs={{0,4},{4,8},{8,12},{12,16},{16,20},{20,24},{24,28},{1,5},{5,9},{9,... | collective-permute-start | bytes 98312 | tf_op jit(solution)/shard_map/ppermute | solution.py:11
  19.2 33.7 %copy-start.1 = (bf16[16,64,128]{2,1,0:T(8,128)(2,1)}, bf16[16,64,128]{2,1,0:T(8,128)(2,1)S(1)}, u32[]{:S(2)}) copy-start(bf16[16,64,128]{2,1,0:T(8,128)(2,1)S(1)} %fusion.4) | copy-start | bytes 786436
Sparse Core Ops, SparseCore 0:
  20.5 28.2 all-gather.8
